TPU v7x, 32 devices: a whole 2x2x4 slice. The times are simulated.
32 devices in a mesh: men: 16 (over z, x, core), women: 2 (over y).
Axes of the slice: x: 2, y: 2, z: 4, core: 2. Of those that a mesh axis runs over, the one named last changes fastest.
Arguments:
- men_traits: bfloat16 [64, 16384], P(None, ('men', 'women')), may hold values from -4 to 4
- women_traits: bfloat16 [64, 8192], P(None, ('women', 'men')), may hold values from -4 to 4
- affinity: float32 [64, 64], replicated, may hold values from -0.375 to 0.375
- observed: float32 [64, 64], replicated, may hold values from -0.25 to 0.25
- men_mass: float32 [16384], P('men'), may hold values from 0.5 to 2
- women_mass: float32 [8192], P('women'), may hold values from 0.5 to 2
Outputs:
- men_scale: float32 [16384], P('men')
- women_scale: float32 [8192], P('women')
- updated: float32 [64, 64], replicated
All inputs are finite; a program needn't handle non-finite values.
Results may differ from a plain program's by a relative error of at most 0.0022.
Values may be sent and summed in bfloat16 or wider, within the bound.
A program may use at most 64 MiB of HBM per device.

v0:
```python
import functools
import math
import jax
import jax.numpy as jnp
from jax import lax
from jax.experimental import pallas as pl
from jax.experimental.pallas import tpu as pltpu
from jax.sharding import PartitionSpec as P

F32, BF16 = jnp.float32, jnp.bfloat16
MESH = pl.DeviceIdType.MESH
LHS_T = (((0,), (0,)), ((), ()))
RHS_T = (((1,), (1,)), ((), ()))


def split3(value):
    high = value.astype(BF16)
    rest = value - high.astype(F32)
    mid = rest.astype(BF16)
    low = (rest - mid.astype(F32)).astype(BF16)
    return high, mid, low


def factors(men):
    cores = 2 if men % 2 == 0 else 1
    chips = men // cores
    planes = 1 << (chips.bit_length() // 2)
    if chips % planes:
        planes = 1
    return planes, chips // planes, cores


def body(dims, ws, men_total, women_total,
         men_ref, women_ref, aff_hbm, obs_hbm, mm_hbm, wm_hbm,
         ms_out, ws_out, up_out,
         men_buf, wom_buf, scaled_ref, e_ref, t_ref, col_ref, rsum_ref, scale_ref,
         aff_ref, obs_ref, wm_ref, mass_buf, wx_buf,
         r_buf, c_buf, mxy_buf, mc_buf, mz_buf,
         own_sem, gm_s, gm_r, gz_s, gz_r, gc_s, gc_r, mm_s, mm_r, wx_s, wx_r,
         rx_s, rx_r, cz_s, cz_r, mc_s, mc_r, mz_s, mz_r):
    zs, xs, cs = dims
    nm, nb = xs * ws, zs * cs
    traits, wb = women_ref.shape
    mb = men_ref.shape[1]
    rows = mm_hbm.shape[1]
    group_rows = nm * mb
    log_count = math.log(women_total)
    mi = lax.axis_index("men")
    yi = lax.axis_index("women")
    ci = lax.rem(mi, cs)
    xi = lax.rem(lax.div(mi, cs), xs)
    zi = lax.div(mi, cs * xs)
    xy_me = xi * ws + yi
    zc_me = ci * zs + zi

    def plus(value, step, size):
        return lax.rem(value + step, size)

    def xy_peer(dx, dy):
        return ((zi * xs + plus(xi, dx, xs)) * cs + ci, plus(yi, dy, ws))

    def zc_peer(dc, dz):
        return ((plus(zi, dz, zs) * xs + xi) * cs + plus(ci, dc, cs), yi)

    xy_ids = [xy_peer(dx, dy) for dx in range(xs) for dy in range(ws) if dx + dy]
    zc_ids = [zc_peer(dc, dz) for dc in range(cs) for dz in range(zs) if dc + dz]
    x_ids = [xy_peer(dx, 0) for dx in range(1, xs)]
    c_ids = [zc_peer(dc, 0) for dc in range(1, cs)]
    z_ids = [zc_peer(0, dz) for dz in range(1, zs)]

    barrier = pltpu.get_barrier_semaphore()
    everyone = xy_ids + zc_ids
    for peer in everyone:
        pl.semaphore_signal(barrier, inc=1, device_id=peer, device_id_type=MESH)
    local = [
        pltpu.make_async_copy(src, dst, own_sem.at[k])
        for k, (src, dst) in enumerate([
            (men_ref, men_buf.at[xy_me]), (women_ref, wom_buf.at[zc_me]), (aff_hbm, aff_ref),
            (mm_hbm, mass_buf.at[xi]), (wm_hbm, wm_ref), (obs_hbm, obs_ref)])
    ]
    for copy in local:
        copy.start()
    pl.semaphore_wait(barrier, len(everyone))

    def remote(src, dst, send, recv, peer):
        return pltpu.make_async_remote_copy(
            src_ref=src, dst_ref=dst, send_sem=send, recv_sem=recv,
            device_id=peer, device_id_type=MESH)

    def z_copy(dz):
        return remote(women_ref, wom_buf.at[zc_me], gz_s.at[dz], gz_r.at[dz], zc_peer(0, dz))

    def c_copy(dz):
        held = wom_buf.at[ci * zs + plus(zi, zs - dz, zs)]
        return remote(held, held, gc_s.at[dz], gc_r.at[dz], zc_peer(1, 0))

    def m_copy(k):
        return remote(men_ref, men_buf.at[xy_me], gm_s.at[k], gm_r.at[k],
                      xy_peer(lax.div(k, ws), lax.rem(k, ws)))

    for dz in range(1, zs):
        z_copy(dz).start()
    for k in range(1, nm):
        m_copy(k).start()
    pending = []
    for k, peer in enumerate(x_ids):
        copy = remote(mm_hbm, mass_buf.at[xi], mm_s.at[k], mm_r.at[k], peer)
        copy.start()
        pending.append(copy)
    mass_copies = list(pending)
    for copy in local:
        copy.wait()
    if cs > 1:
        c_copy(0).start()

    def shard_of(k):
        return plus(xi, xs - lax.div(k, ws), xs) * ws + plus(yi, ws - lax.rem(k, ws), ws)

    def rows_of(shard):
        return pl.ds(pl.multiple_of(shard * mb, mb), mb)

    def make_scaled(shard):
        high, mid, low = [
            lax.dot_general(men_buf[shard], part, LHS_T, preferred_element_type=F32)
            for part in split3(aff_ref[...])
        ]
        scaled_ref[rows_of(shard), :] = ((low + mid) + high).astype(BF16)

    make_scaled(xy_me)
    tile = math.gcd(mb, 256)
    fold = wb // 128 if wb % 128 == 0 else 1
    lanes = wb // fold
    rsum_ref[...] = jnp.zeros_like(rsum_ref)

    def fill(q, start, count):
        block = wom_buf[q]
        for part in range(count):
            at = pl.ds(pl.multiple_of(start + part * tile, tile), tile)
            surplus = jnp.dot(scaled_ref[at, :], block, preferred_element_type=F32)
            kernel = jnp.exp(surplus - log_count)
            e_ref[q, at, :] = kernel.astype(BF16)
            total = rsum_ref[at, :]
            for piece in range(fold):
                total = total + kernel[:, piece * lanes:(piece + 1) * lanes]
            rsum_ref[at, :] = total

    def z_block(dz):
        return ci * zs + plus(zi, zs - dz, zs)

    fill(zc_me, xy_me * mb, mb // tile)

    def own_men(dz, carry):
        z_copy(dz).wait_recv()
        if cs > 1:
            c_copy(dz).start()
        fill(z_block(dz), xy_me * mb, mb // tile)
        return carry

    def other_men(k, carry):
        m_copy(k).wait_recv()
        shard = shard_of(k)
        make_scaled(shard)
        for z in range(zs):
            fill(ci * zs + z, shard * mb, mb // tile)
        return carry

    def other_core(dz, carry):
        c_copy(dz).wait_recv()
        fill(plus(ci, 1, cs) * zs + plus(zi, zs - dz, zs), 0, group_rows // tile)
        return carry

    lax.fori_loop(1, zs, own_men, 0)
    lax.fori_loop(1, nm, other_men, 0)
    if cs > 1:
        lax.fori_loop(0, zs, other_core, 0)

    def group_sum(value, buf, me, send, recv, peers):
        if not peers:
            return value
        buf[me] = value
        copies = []
        for k, peer in enumerate(peers):
            copy = remote(buf.at[me], buf.at[me], send.at[k], recv.at[k], peer)
            copy.start()
            copies.append(copy)
        for copy in copies:
            copy.wait_recv()
        pending.extend(copies)
        total = buf[0]
        for slot in range(1, buf.shape[0]):
            total = total + buf[slot]
        return total

    for copy in mass_copies:
        copy.wait_recv()
    men_mass = jnp.concatenate([mass_buf[x] for x in range(xs)], axis=1)
    men_full = jnp.concatenate([men_buf[k] for k in range(nm)], axis=1)
    mass_q = None
    for x in range(xs):
        order = [(z * xs + x) * cs + c for c in range(cs) for z in range(zs)]
        mine = jnp.concatenate([wm_ref[:, p * wb:(p + 1) * wb] for p in order], axis=0)
        mass_q = mine if mass_q is None else jnp.where(xi == x, mine, mass_q)

    def men_update(it, row_sum):
        return men_mass / group_sum(row_sum, r_buf.at[it], xy_me, rx_s.at[it], rx_r.at[it], xy_ids)

    def women_update(it, partial):
        return mass_q / group_sum(partial, c_buf.at[it], zc_me, cz_s.at[it], cz_r.at[it], zc_ids)

    zeros13 = jnp.zeros((13, group_rows), BF16)
    zeros13w = jnp.zeros((13, wb), BF16)

    def sweep(step, carry):
        for q in range(nb):
            carry = step(q, carry)
        return carry

    sums = rsum_ref[...]
    high = sums.astype(BF16)
    low = (sums - high.astype(F32)).astype(BF16)
    total = lax.dot_general(jnp.ones((16, 2 * lanes), BF16), jnp.concatenate([high, low], axis=1),
                            RHS_T, preferred_element_type=F32)
    scale = men_update(0, total[0:1])
    left0 = jnp.concatenate(list(split3(scale)) + [zeros13], axis=0)

    def col_step(q, carry):
        out = jnp.dot(left0, e_ref[q], preferred_element_type=F32)
        col_ref[q:q + 1, :] = out[0:1] + out[1:2] + out[2:3]
        return carry

    sweep(col_step, 0)
    col_ref[...] = women_update(0, col_ref[...])

    def row_step(q, total):
        lines = jnp.concatenate(list(split3(col_ref[q:q + 1, :])) + [zeros13w], axis=0)
        return total + lax.dot_general(lines, e_ref[q], RHS_T, preferred_element_type=F32)

    total = sweep(row_step, jnp.zeros((16, group_rows), F32))
    scale = men_update(1, total[0:1] + total[1:2] + total[2:3])
    for x in range(xs):
        scale_ref[x] = scale[:, x * rows:(x + 1) * rows]
    ms_out[...] = scale_ref[xi]

    weighted = (men_full.astype(F32) * scale).astype(BF16)
    left = jnp.concatenate([weighted] + list(split3(scale)) + [zeros13], axis=0)

    def both_step(q, carry):
        out = jnp.dot(left, e_ref[q], preferred_element_type=F32)
        t_ref[q] = out[0:traits]
        col_ref[q:q + 1, :] = (out[traits:traits + 1] + out[traits + 1:traits + 2]
                               + out[traits + 2:traits + 3])
        return carry

    sweep(both_step, 0)
    women_scale = women_update(1, col_ref[...])
    col_ref[...] = women_scale
    wx_buf[xi] = women_scale
    wx_copies = []
    for k, peer in enumerate(x_ids):
        copy = remote(wx_buf.at[xi], wx_buf.at[xi], wx_s.at[k], wx_r.at[k], peer)
        copy.start()
        wx_copies.append(copy)
    pending.extend(wx_copies)

    def moment_step(q, moment):
        inner = t_ref[q] * col_ref[q:q + 1, :]
        high = inner.astype(BF16)
        low = (inner - high.astype(F32)).astype(BF16)
        both = jnp.concatenate([high, low], axis=0)
        return moment + lax.dot_general(both, wom_buf[q], RHS_T, preferred_element_type=F32)

    moment = sweep(moment_step, jnp.zeros((2 * traits, traits), F32))
    moment = moment[0:traits] + moment[traits:]
    half = traits // 2
    packed = jnp.concatenate([moment[0:half], moment[half:]], axis=1)
    packed = group_sum(packed, mxy_buf, xy_me, rx_s.at[2], rx_r.at[2], xy_ids)
    packed = group_sum(packed, mc_buf, ci, mc_s, mc_r, c_ids)
    for copy in wx_copies:
        copy.wait_recv()
    for x in range(xs):
        scales = wx_buf[x]
        for q in range(nb):
            p = ((q % zs) * xs + x) * cs + q // zs
            ws_out[:, p * wb:(p + 1) * wb] = scales[q:q + 1, :]
    packed = group_sum(packed, mz_buf, zi, mz_s, mz_r, z_ids)
    moment = jnp.concatenate([packed[:, 0:traits], packed[:, traits:]], axis=0)
    up_out[...] = aff_ref[...] + obs_ref[...] - moment * (1.0 / men_total)

    for copy in pending:
        copy.wait_send()
    for dz in range(1, zs):
        z_copy(dz).wait_send()
    for k in range(1, nm):
        m_copy(k).wait_send()
    if cs > 1:
        for dz in range(zs):
            c_copy(dz).wait_send()


def solution(mesh):
    men_axis, women_axis = mesh.shape["men"], mesh.shape["women"]
    dims = factors(men_axis)
    zs, xs, cs = dims

    def on_device(men_traits, women_traits, affinity, observed, men_mass, women_mass):
        traits, mb = men_traits.shape
        wb = women_traits.shape[1]
        rows, cols = men_mass.shape[0], women_mass.shape[0]
        nm, nb = xs * women_axis, zs * cs
        dma = pltpu.SemaphoreType.DMA
        vmem = pl.BlockSpec(memory_space=pltpu.VMEM)
        anywhere = pl.BlockSpec(memory_space=pl.ANY)
        packed = (traits // 2, 2 * traits)
        out = pl.pallas_call(
            functools.partial(body, dims, women_axis, rows * men_axis, cols * women_axis),
            out_shape=(
                jax.ShapeDtypeStruct((1, rows), F32),
                jax.ShapeDtypeStruct((1, cols), F32),
                jax.ShapeDtypeStruct((traits, traits), F32),
            ),
            in_specs=[anywhere] * 6,
            out_specs=(vmem, vmem, vmem),
            scratch_shapes=[
                pltpu.VMEM((nm, traits, mb), BF16),
                pltpu.VMEM((nb, traits, wb), BF16),
                pltpu.VMEM((nm * mb, traits), BF16),
                pltpu.VMEM((nb, nm * mb, wb), BF16),
                pltpu.VMEM((nb, traits, wb), F32),
                pltpu.VMEM((nb, wb), F32),
                pltpu.VMEM((nm * mb, wb if wb % 128 else 128), F32),
                pltpu.VMEM((xs, 1, rows), F32),
                pltpu.VMEM((traits, traits), F32),
                pltpu.VMEM((traits, traits), F32),
                pltpu.VMEM((1, cols), F32),
                pltpu.VMEM((xs, 1, rows), F32),
                pltpu.VMEM((xs, nb, wb), F32),
                pltpu.VMEM((2, nm, 1, nm * mb), F32),
                pltpu.VMEM((2, nb, nb, wb), F32),
                pltpu.VMEM((nm,) + packed, F32),
                pltpu.VMEM((cs,) + packed, F32),
                pltpu.VMEM((zs,) + packed, F32),
                dma((6,)),
                dma((nm,)), dma((nm,)),
                dma((zs,)), dma((zs,)),
                dma((zs,)), dma((zs,)),
                dma((xs,)), dma((xs,)),
                dma((xs,)), dma((xs,)),
                dma((3, nm)), dma((3, nm)),
                dma((2, nb)), dma((2, nb)),
                dma((cs,)), dma((cs,)),
                dma((zs,)), dma((zs,)),
            ],
            compiler_params=pltpu.CompilerParams(
                collective_id=0, has_side_effects=True, vmem_limit_bytes=60 * 1024 * 1024),
        )(men_traits, women_traits, affinity, observed,
          men_mass.reshape(1, rows), women_mass.reshape(1, cols))
        return out[0].reshape(rows), out[1].reshape(cols), out[2]

    placed = (P(None, ("men", "women")), P(None, ("women", "men")), P(), P(), P("men"), P("women"))
    return jax.shard_map(
        on_device,
        mesh=mesh,
        in_specs=placed,
        out_specs=(P("men"), P("women"), P()),
        check_vma=False,
    )
```

profile of v0, /device:TPU:0, one launch (start us, length us, event | category | flops | bytes accessed | tf_op | source)
XLA Modules:
  0.0 48.2 jit_solution(10509053105829647735)
XLA Ops:
  0.6 44.4 %shard_map.85 = (f32[1,1024]{1,0:T(1,128)}, f32[1,4096]{1,0:T(1,128)}, f32[64,64]{1,0:T(8,128)}) custom-call(bf16[64,512]{1,0:T(8,128)(2,1)} %men_ref.1, bf16[64,256]{1,0:T(8,128)(2,1)} %women_ref.1, f32[64,64]{1,0:T(8,128)} %aff_hbm.1, f32[64,64]{1,0:T(8,128)} %obs_hbm.1, f32[1,1024]{1,0:T(1,128)} %bitcast.6, f32[1,4096]{1,0:T(1,128)} %bitcast.4), custom_call_target="tpu_custom_call" | custom-call | tf_op jit(solution)/shard_map/pallas_call | solution.py:314
  45.0 0.0 copy-start
  45.0 1.3 %copy.12 = f32[1024]{0:T(1024)} copy(f32[1024]{0:T(1024)} %bitcast.7) | data formatting | bytes 8192
  46.3 1.3 %copy.13 = f32[4096]{0:T(1024)} copy(f32[4096]{0:T(1024)} %bitcast.5) | data formatting | bytes 32768
  47.6 0.0 copy-done
  47.6 0.6 %copy.14 = f32[64,64]{1,0:T(8,128)} copy(f32[64,64]{1,0:T(8,128)S(1)} %copy-done) | data formatting | bytes 32768
Async XLA Ops:
  45.0 2.6 %copy-start = (f32[64,64]{1,0:T(8,128)S(1)}, f32[64,64]{1,0:T(8,128)}, u32[]{:S(2)}) copy-start(f32[64,64]{1,0:T(8,128)} %get-tuple-element.14) | copy-start | bytes 49156
where the time goes:
time: 48.5 us; the launch traced here: 48.2 us
  Pallas kernels  44.4 us (92%)
  local copies, waits for them, and re-layouts  3.22 us (7%)
  between operations  0.65 us (1%)
    pallas_call x1, Pallas kernels, on_device(): pl.pallas_call(functools.partial(body, dims, women_axis, rows * men_axis,...  44.4 us
    unnamed x5, local copies, waits for them, and re-layouts  3.22 us

commit v1 on v0

--- a/solution.py
+++ b/solution.py
@@ -2,6 +2,8 @@
 import math
 import jax
 import jax.numpy as jnp
+import ml_dtypes
+import numpy as np
 from jax import lax
 from jax.experimental import pallas as pl
 from jax.experimental.pallas import tpu as pltpu
@@ -41,6 +43,7 @@
     zs, xs, cs = dims
     nm, nb = xs * ws, zs * cs
     traits, wb = women_ref.shape
+    deep = wom_buf.shape[1]
     mb = men_ref.shape[1]
     rows = mm_hbm.shape[1]
     group_rows = nm * mb
@@ -62,6 +65,9 @@
     def zc_peer(dc, dz):
         return ((plus(zi, dz, zs) * xs + xi) * cs + plus(ci, dc, cs), yi)
 
+    def traits_of(q):
+        return wom_buf.at[q, pl.ds(0, traits)]
+
     xy_ids = [xy_peer(dx, dy) for dx in range(xs) for dy in range(ws) if dx + dy]
     zc_ids = [zc_peer(dc, dz) for dc in range(cs) for dz in range(zs) if dc + dz]
     x_ids = [xy_peer(dx, 0) for dx in range(1, xs)]
@@ -75,29 +81,86 @@
     local = [
         pltpu.make_async_copy(src, dst, own_sem.at[k])
         for k, (src, dst) in enumerate([
-            (men_ref, men_buf.at[xy_me]), (women_ref, wom_buf.at[zc_me]), (aff_hbm, aff_ref),
+            (men_ref, men_buf.at[xy_me]), (women_ref, traits_of(zc_me)), (aff_hbm, aff_ref),
             (mm_hbm, mass_buf.at[xi]), (wm_hbm, wm_ref), (obs_hbm, obs_ref)])
     ]
     for copy in local:
         copy.start()
-    pl.semaphore_wait(barrier, len(everyone))
-
     def remote(src, dst, send, recv, peer):
         return pltpu.make_async_remote_copy(
             src_ref=src, dst_ref=dst, send_sem=send, recv_sem=recv,
             device_id=peer, device_id_type=MESH)
 
     def z_copy(dz):
-        return remote(women_ref, wom_buf.at[zc_me], gz_s.at[dz], gz_r.at[dz], zc_peer(0, dz))
+        return remote(women_ref, traits_of(zc_me), gz_s.at[dz], gz_r.at[dz], zc_peer(0, dz))
+
+    def source_z(dz):
+        return plus(zi, zs - dz, zs)
 
     def c_copy(dz):
-        held = wom_buf.at[ci * zs + plus(zi, zs - dz, zs)]
+        held = traits_of(ci * zs + source_z(dz))
         return remote(held, held, gc_s.at[dz], gc_r.at[dz], zc_peer(1, 0))
 
     def m_copy(k):
         return remote(men_ref, men_buf.at[xy_me], gm_s.at[k], gm_r.at[k],
                       xy_peer(lax.div(k, ws), lax.rem(k, ws)))
 
+    def shard_of(k):
+        return plus(xi, xs - lax.div(k, ws), xs) * ws + plus(yi, ws - lax.rem(k, ws), ws)
+
+    def rows_of(shard):
+        return pl.ds(pl.multiple_of(shard * mb, mb), mb)
+
+    column = lax.broadcasted_iota(jnp.int32, (1, deep), 1)
+    ones_row = jnp.where((column >= traits) & (column < traits + 3), 1.0, 0.0).astype(F32)
+    line = lax.broadcasted_iota(jnp.int32, (deep - traits, wb), 0)
+    tail = jnp.zeros((deep - traits, wb), F32)
+    rest = log_count
+    for step in range(3):
+        piece = float(np.asarray(rest, ml_dtypes.bfloat16))
+        tail = jnp.where(line == step, -piece, tail)
+        rest -= piece
+    tail = tail.astype(BF16)
+    for q in range(nb):
+        wom_buf[q, traits:] = tail
+    rsum_ref[...] = jnp.zeros_like(rsum_ref)
+    tile = math.gcd(mb, 256)
+    fold = wb // 128 if wb % 128 == 0 else 1
+    lanes = wb // fold
+
+    def make_scaled(shard):
+        wide = jnp.concatenate([aff_ref[...], jnp.zeros((traits, deep - traits), F32)], axis=1)
+        high, mid, low = [
+            lax.dot_general(men_buf[shard], part, LHS_T, preferred_element_type=F32)
+            for part in split3(wide)
+        ]
+        scaled_ref[rows_of(shard), :] = (((low + mid) + high) + ones_row).astype(BF16)
+
+    def fill(blocks, start, count):
+        for part in range(count):
+            at = pl.ds(pl.multiple_of(start + part * tile, tile), tile)
+            total = None
+            for q in blocks:
+                surplus = jnp.dot(scaled_ref[at, :], wom_buf[q], preferred_element_type=F32)
+                kernel = jnp.exp(surplus)
+                e_ref[q, at, :] = kernel.astype(BF16)
+                for piece in range(fold):
+                    term = kernel[:, piece * lanes:(piece + 1) * lanes]
+                    total = term if total is None else total + term
+            rsum_ref[at, :] += total
+
+    def fill_men(blocks, ks):
+        for k in ks:
+            fill(blocks, shard_of(k) * mb, mb // tile)
+
+    for copy in local:
+        copy.wait()
+    make_scaled(xy_me)
+    fill([zc_me], xy_me * mb, mb // tile)
+
+    pl.semaphore_wait(barrier, len(everyone))
+    if cs > 1:
+        c_copy(0).start()
     for dz in range(1, zs):
         z_copy(dz).start()
     for k in range(1, nm):
@@ -108,71 +171,75 @@
         copy.start()
         pending.append(copy)
     mass_copies = list(pending)
-    for copy in local:
-        copy.wait()
-    if cs > 1:
-        c_copy(0).start()
-
-    def shard_of(k):
-        return plus(xi, xs - lax.div(k, ws), xs) * ws + plus(yi, ws - lax.rem(k, ws), ws)
-
-    def rows_of(shard):
-        return pl.ds(pl.multiple_of(shard * mb, mb), mb)
-
-    def make_scaled(shard):
-        high, mid, low = [
-            lax.dot_general(men_buf[shard], part, LHS_T, preferred_element_type=F32)
-            for part in split3(aff_ref[...])
-        ]
-        scaled_ref[rows_of(shard), :] = ((low + mid) + high).astype(BF16)
-
-    make_scaled(xy_me)
-    tile = math.gcd(mb, 256)
-    fold = wb // 128 if wb % 128 == 0 else 1
-    lanes = wb // fold
-    rsum_ref[...] = jnp.zeros_like(rsum_ref)
-
-    def fill(q, start, count):
-        block = wom_buf[q]
-        for part in range(count):
-            at = pl.ds(pl.multiple_of(start + part * tile, tile), tile)
-            surplus = jnp.dot(scaled_ref[at, :], block, preferred_element_type=F32)
-            kernel = jnp.exp(surplus - log_count)
-            e_ref[q, at, :] = kernel.astype(BF16)
-            total = rsum_ref[at, :]
-            for piece in range(fold):
-                total = total + kernel[:, piece * lanes:(piece + 1) * lanes]
-            rsum_ref[at, :] = total
-
-    def z_block(dz):
-        return ci * zs + plus(zi, zs - dz, zs)
-
-    fill(zc_me, xy_me * mb, mb // tile)
-
-    def own_men(dz, carry):
-        z_copy(dz).wait_recv()
+
+    def step_of(n):
+        near = [sorted(range(zs), key=lambda z: (abs(z - own), -z))[n] for own in range(zs)]
+        steps = [(own - z) % zs for own, z in enumerate(near)]
+        value = jnp.int32(steps[0])
+        for own in range(1, zs):
+            value = jnp.where(zi == own, steps[own], value)
+        return value
+
+    def own_block(n):
+        return ci * zs + source_z(order[n])
+
+    def twin_block(n):
+        return plus(ci, 1, cs) * zs + source_z(order[n])
+
+    order = [0] + [step_of(n) for n in range(1, zs)]
+    if cs == 2 and nm == 4 and zs == 4:
+        def take_z(n):
+            z_copy(order[n]).wait_recv()
+            c_copy(order[n]).start()
+
+        def take_men(k):
+            m_copy(k).wait_recv()
+            make_scaled(shard_of(k))
+
+        c_copy(0).wait_recv()
+        fill_men([twin_block(0)], [0])
+        take_z(1)
+        fill_men([own_block(1)], [0])
+        take_men(1)
+        fill_men([own_block(0), twin_block(0), own_block(1)], [1])
+        take_z(2)
+        c_copy(order[1]).wait_recv()
+        fill_men([twin_block(1)], [0, 1])
+        take_men(2)
+        fill_men([own_block(0), twin_block(0), own_block(1), twin_block(1)], [2])
+        take_z(3)
+        fill_men([own_block(2)], [0, 1, 2])
+        take_men(3)
+        fill_men([own_block(0), twin_block(0), own_block(1), twin_block(1), own_block(2)], [3])
+        c_copy(order[2]).wait_recv()
+        fill([twin_block(2), own_block(3)], 0, group_rows // tile)
+        c_copy(order[3]).wait_recv()
+        fill([twin_block(3)], 0, group_rows // tile)
+    else:
+        def own_men(dz, carry):
+            z_copy(dz).wait_recv()
+            if cs > 1:
+                c_copy(dz).start()
+            fill([ci * zs + source_z(dz)], xy_me * mb, mb // tile)
+            return carry
+
+        def other_men(k, carry):
+            m_copy(k).wait_recv()
+            shard = shard_of(k)
+            make_scaled(shard)
+            for z in range(zs):
+                fill([ci * zs + z], shard * mb, mb // tile)
+            return carry
+
+        def other_core(dz, carry):
+            c_copy(dz).wait_recv()
+            fill([plus(ci, 1, cs) * zs + source_z(dz)], 0, group_rows // tile)
+            return carry
+
+        lax.fori_loop(1, zs, own_men, 0)
+        lax.fori_loop(1, nm, other_men, 0)
         if cs > 1:
-            c_copy(dz).start()
-        fill(z_block(dz), xy_me * mb, mb // tile)
-        return carry
-
-    def other_men(k, carry):
-        m_copy(k).wait_recv()
-        shard = shard_of(k)
-        make_scaled(shard)
-        for z in range(zs):
-            fill(ci * zs + z, shard * mb, mb // tile)
-        return carry
-
-    def other_core(dz, carry):
-        c_copy(dz).wait_recv()
-        fill(plus(ci, 1, cs) * zs + plus(zi, zs - dz, zs), 0, group_rows // tile)
-        return carry
-
-    lax.fori_loop(1, zs, own_men, 0)
-    lax.fori_loop(1, nm, other_men, 0)
-    if cs > 1:
-        lax.fori_loop(0, zs, other_core, 0)
+            lax.fori_loop(0, zs, other_core, 0)
 
     def group_sum(value, buf, me, send, recv, peers):
         if not peers:
@@ -267,7 +334,7 @@
         high = inner.astype(BF16)
         low = (inner - high.astype(F32)).astype(BF16)
         both = jnp.concatenate([high, low], axis=0)
-        return moment + lax.dot_general(both, wom_buf[q], RHS_T, preferred_element_type=F32)
+        return moment + lax.dot_general(both, wom_buf[q, 0:traits], RHS_T, preferred_element_type=F32)
 
     moment = sweep(moment_step, jnp.zeros((2 * traits, traits), F32))
     moment = moment[0:traits] + moment[traits:]
@@ -297,6 +364,17 @@
             c_copy(dz).wait_send()
 
 
+def deliver(ms_ref, ws_ref, up_ref, ms_out, ws_out, up_out, sems):
+    copies = [
+        pltpu.make_async_copy(src, dst, sems.at[k])
+        for k, (src, dst) in enumerate([(ms_ref, ms_out), (ws_ref, ws_out), (up_ref, up_out)])
+    ]
+    for copy in copies:
+        copy.start()
+    for copy in copies:
+        copy.wait()
+
+
 def solution(mesh):
     men_axis, women_axis = mesh.shape["men"], mesh.shape["women"]
     dims = factors(men_axis)
@@ -307,6 +385,7 @@
         wb = women_traits.shape[1]
         rows, cols = men_mass.shape[0], women_mass.shape[0]
         nm, nb = xs * women_axis, zs * cs
+        deep = traits + 16
         dma = pltpu.SemaphoreType.DMA
         vmem = pl.BlockSpec(memory_space=pltpu.VMEM)
         anywhere = pl.BlockSpec(memory_space=pl.ANY)
@@ -314,16 +393,16 @@
         out = pl.pallas_call(
             functools.partial(body, dims, women_axis, rows * men_axis, cols * women_axis),
             out_shape=(
-                jax.ShapeDtypeStruct((1, rows), F32),
-                jax.ShapeDtypeStruct((1, cols), F32),
-                jax.ShapeDtypeStruct((traits, traits), F32),
+                pltpu.VMEM((1, rows), F32),
+                pltpu.VMEM((1, cols), F32),
+                pltpu.VMEM((traits, traits), F32),
             ),
             in_specs=[anywhere] * 6,
             out_specs=(vmem, vmem, vmem),
             scratch_shapes=[
                 pltpu.VMEM((nm, traits, mb), BF16),
-                pltpu.VMEM((nb, traits, wb), BF16),
-                pltpu.VMEM((nm * mb, traits), BF16),
+                pltpu.VMEM((nb, deep, wb), BF16),
+                pltpu.VMEM((nm * mb, deep), BF16),
                 pltpu.VMEM((nb, nm * mb, wb), BF16),
                 pltpu.VMEM((nb, traits, wb), F32),
                 pltpu.VMEM((nb, wb), F32),
@@ -354,6 +433,17 @@
                 collective_id=0, has_side_effects=True, vmem_limit_bytes=60 * 1024 * 1024),
         )(men_traits, women_traits, affinity, observed,
           men_mass.reshape(1, rows), women_mass.reshape(1, cols))
+        out = pl.pallas_call(
+            deliver,
+            out_shape=(
+                jax.ShapeDtypeStruct((1, rows), F32),
+                jax.ShapeDtypeStruct((1, cols), F32),
+                jax.ShapeDtypeStruct((traits, traits), F32),
+            ),
+            in_specs=[vmem] * 3,
+            out_specs=(anywhere,) * 3,
+            scratch_shapes=[dma((3,))],
+        )(*[pltpu.with_memory_space_constraint(value, pltpu.VMEM) for value in out])
         return out[0].reshape(rows), out[1].reshape(cols), out[2]
 
     placed = (P(None, ("men", "women")), P(None, ("women", "men")), P(), P(), P("men"), P("women"))

time: 48.5 us -> 43.3 us (0.89)
  local copies, waits for them, and re-layouts: 3.22 us -> 0 us
  Pallas kernels: 44.4 us -> 42.5 us
    unnamed x5 -> x0, local copies, waits for them, and re-layouts: 3.22 us -> none
    pallas_call x1, Pallas kernels: 44.4 us -> 41.8 us  [on_device(): pl.pallas_call(functools.partial(body, dims, women_axis, rows * men_axis,...]
    pallas_call x0 -> x1, Pallas kernels: none -> 0.65 us  [on_device(): pl.pallas_call(deliver, out_shape=(jax.ShapeDtypeStruct((1, rows), F32),...]
where the time goes in v1:
time: 43.3 us; the launch traced here: 43.1 us
  Pallas kernels  42.5 us (98%)
  between operations  0.64 us (1%)
    pallas_call x1, Pallas kernels, on_device(): pl.pallas_call(functools.partial(body, dims, women_axis, rows * men_axis,...  41.8 us

profile of v1, /device:TPU:0, one launch (start us, length us, event | category | flops | bytes accessed | tf_op | source)
XLA Modules:
  0.0 43.1 jit_solution(14630819713234107089)
XLA Ops:
  0.6 41.8 %shard_map.85 = (f32[1,1024]{1,0:T(1,128)S(1)}, f32[1,4096]{1,0:T(1,128)S(1)}, f32[64,64]{1,0:T(8,128)S(1)}) custom-call(bf16[64,512]{1,0:T(8,128)(2,1)} %men_ref.1, bf16[64,256]{1,0:T(8,128)(2,1)} %women_ref.1, f32[64,64]{1,0:T(8,128)} %aff_hbm.1, f32[64,64]{1,0:T(8,128)} %obs_hbm.1, f32[1,1024]{1,0:T(1,128)} %bitcast.5, f32[1,4096]{1,0:T(1,128)} %bitcast.4), custom_call_target="tpu_custom_call" | custom-call | tf_op jit(solution)/shard_map/pallas_call | solution.py:393
  42.4 0.7 %shard_map.86 = (f32[1,1024]{1,0:T(1,128)}, f32[1,4096]{1,0:T(1,128)}, f32[64,64]{1,0:T(8,128)}) custom-call(f32[1,1024]{1,0:T(1,128)S(1)} %get-tuple-element.9.ms_ref, f32[1,4096]{1,0:T(1,128)S(1)} %get-tuple-element.10.ws_ref, f32[64,64]{1,0:T(8,128)S(1)} %get-tuple-element.11.up_ref), custom_call_target="tpu_custom_call" | custom-call | tf_op jit(solution)/shard_map/pallas_call | solution.py:436

commit v2 on v1

--- a/solution.py
+++ b/solution.py
@@ -36,10 +36,10 @@
          men_ref, women_ref, aff_hbm, obs_hbm, mm_hbm, wm_hbm,
          ms_out, ws_out, up_out,
          men_buf, wom_buf, scaled_ref, e_ref, t_ref, col_ref, rsum_ref, scale_ref,
-         aff_ref, obs_ref, wm_ref, mass_buf, wx_buf,
-         r_buf, c_buf, mxy_buf, mc_buf, mz_buf,
+         left_aff, aff_ref, obs_ref, wm_ref, mass_buf, wx_buf,
+         r_buf, c_buf, mxy_buf, mz_buf, t_in,
          own_sem, gm_s, gm_r, gz_s, gz_r, gc_s, gc_r, mm_s, mm_r, wx_s, wx_r,
-         rx_s, rx_r, cz_s, cz_r, mc_s, mc_r, mz_s, mz_r):
+         rx_s, rx_r, cz_s, cz_r, tx_s, tx_r, mz_s, mz_r):
     zs, xs, cs = dims
     nm, nb = xs * ws, zs * cs
     traits, wb = women_ref.shape
@@ -71,8 +71,6 @@
     xy_ids = [xy_peer(dx, dy) for dx in range(xs) for dy in range(ws) if dx + dy]
     zc_ids = [zc_peer(dc, dz) for dc in range(cs) for dz in range(zs) if dc + dz]
     x_ids = [xy_peer(dx, 0) for dx in range(1, xs)]
-    c_ids = [zc_peer(dc, 0) for dc in range(1, cs)]
-    z_ids = [zc_peer(0, dz) for dz in range(1, zs)]
 
     barrier = pltpu.get_barrier_semaphore()
     everyone = xy_ids + zc_ids
@@ -105,36 +103,47 @@
         return remote(men_ref, men_buf.at[xy_me], gm_s.at[k], gm_r.at[k],
                       xy_peer(lax.div(k, ws), lax.rem(k, ws)))
 
+    def by_distance(sign):
+        order = [0]
+        for n in range(1, zs):
+            near = [sorted(range(zs), key=lambda z: (abs(z - own), -z))[n] for own in range(zs)]
+            steps = [sign * (z - own) % zs for own, z in enumerate(near)]
+            value = jnp.int32(steps[0])
+            for own in range(1, zs):
+                value = jnp.where(zi == own, steps[own], value)
+            order.append(value)
+        return order
+
+    order, send_order = by_distance(-1), by_distance(1)
+    first_copy = remote(women_ref, traits_of(zc_me), gc_s.at[0], gc_r.at[0], zc_peer(1, 0)) if cs > 1 else None
+    pl.semaphore_wait(barrier, len(everyone))
+    if cs > 1:
+        first_copy.start()
+    for n in range(1, zs):
+        z_copy(send_order[n]).start()
+    for k in range(1, nm):
+        m_copy(k).start()
+    pending = []
+    for k, peer in enumerate(x_ids):
+        copy = remote(mm_hbm, mass_buf.at[xi], mm_s.at[k], mm_r.at[k], peer)
+        copy.start()
+        pending.append(copy)
+    mass_copies = list(pending)
+
     def shard_of(k):
         return plus(xi, xs - lax.div(k, ws), xs) * ws + plus(yi, ws - lax.rem(k, ws), ws)
 
     def rows_of(shard):
         return pl.ds(pl.multiple_of(shard * mb, mb), mb)
 
-    column = lax.broadcasted_iota(jnp.int32, (1, deep), 1)
-    ones_row = jnp.where((column >= traits) & (column < traits + 3), 1.0, 0.0).astype(F32)
-    line = lax.broadcasted_iota(jnp.int32, (deep - traits, wb), 0)
-    tail = jnp.zeros((deep - traits, wb), F32)
-    rest = log_count
-    for step in range(3):
-        piece = float(np.asarray(rest, ml_dtypes.bfloat16))
-        tail = jnp.where(line == step, -piece, tail)
-        rest -= piece
-    tail = tail.astype(BF16)
-    for q in range(nb):
-        wom_buf[q, traits:] = tail
-    rsum_ref[...] = jnp.zeros_like(rsum_ref)
     tile = math.gcd(mb, 256)
     fold = wb // 128 if wb % 128 == 0 else 1
     lanes = wb // fold
 
     def make_scaled(shard):
-        wide = jnp.concatenate([aff_ref[...], jnp.zeros((traits, deep - traits), F32)], axis=1)
-        high, mid, low = [
-            lax.dot_general(men_buf[shard], part, LHS_T, preferred_element_type=F32)
-            for part in split3(wide)
-        ]
-        scaled_ref[rows_of(shard), :] = (((low + mid) + high) + ones_row).astype(BF16)
+        block = men_buf[shard]
+        tall = jnp.dot(left_aff[...], jnp.concatenate([block] * 3, axis=0), preferred_element_type=F32)
+        scaled_ref[rows_of(shard), :] = jnp.transpose(tall + ones_column).astype(BF16)
 
     def fill(blocks, start, count):
         for part in range(count):
@@ -153,40 +162,32 @@
         for k in ks:
             fill(blocks, shard_of(k) * mb, mb // tile)
 
+    place = lax.broadcasted_iota(jnp.int32, (deep, 1), 0)
+    ones_column = jnp.where((place >= traits) & (place < traits + 3), 1.0, 0.0).astype(F32)
+    line = lax.broadcasted_iota(jnp.int32, (deep - traits, wb), 0)
+    tail = jnp.zeros((deep - traits, wb), F32)
+    rest = log_count
+    for step in range(3):
+        piece = float(np.asarray(rest, ml_dtypes.bfloat16))
+        tail = jnp.where(line == step, -piece, tail)
+        rest -= piece
+    tail = tail.astype(BF16)
+    for q in range(nb):
+        wom_buf[q, traits:] = tail
+    rsum_ref[...] = jnp.zeros_like(rsum_ref)
     for copy in local:
         copy.wait()
+    wide = jnp.concatenate(split3(jnp.transpose(aff_ref[...])), axis=1)
+    left_aff[...] = jnp.concatenate([wide, jnp.zeros((deep - traits, 3 * traits), BF16)], axis=0)
     make_scaled(xy_me)
     fill([zc_me], xy_me * mb, mb // tile)
 
-    pl.semaphore_wait(barrier, len(everyone))
-    if cs > 1:
-        c_copy(0).start()
-    for dz in range(1, zs):
-        z_copy(dz).start()
-    for k in range(1, nm):
-        m_copy(k).start()
-    pending = []
-    for k, peer in enumerate(x_ids):
-        copy = remote(mm_hbm, mass_buf.at[xi], mm_s.at[k], mm_r.at[k], peer)
-        copy.start()
-        pending.append(copy)
-    mass_copies = list(pending)
-
-    def step_of(n):
-        near = [sorted(range(zs), key=lambda z: (abs(z - own), -z))[n] for own in range(zs)]
-        steps = [(own - z) % zs for own, z in enumerate(near)]
-        value = jnp.int32(steps[0])
-        for own in range(1, zs):
-            value = jnp.where(zi == own, steps[own], value)
-        return value
-
     def own_block(n):
         return ci * zs + source_z(order[n])
 
     def twin_block(n):
         return plus(ci, 1, cs) * zs + source_z(order[n])
 
-    order = [0] + [step_of(n) for n in range(1, zs)]
     if cs == 2 and nm == 4 and zs == 4:
         def take_z(n):
             z_copy(order[n]).wait_recv()
@@ -200,13 +201,13 @@
         fill_men([twin_block(0)], [0])
         take_z(1)
         fill_men([own_block(1)], [0])
-        take_men(1)
-        fill_men([own_block(0), twin_block(0), own_block(1)], [1])
+        take_men(2)
+        fill_men([own_block(0), twin_block(0), own_block(1)], [2])
         take_z(2)
         c_copy(order[1]).wait_recv()
-        fill_men([twin_block(1)], [0, 1])
-        take_men(2)
-        fill_men([own_block(0), twin_block(0), own_block(1), twin_block(1)], [2])
+        fill_men([twin_block(1)], [0, 2])
+        take_men(1)
+        fill_men([own_block(0), twin_block(0), own_block(1), twin_block(1)], [1])
         take_z(3)
         fill_men([own_block(2)], [0, 1, 2])
         take_men(3)
@@ -241,22 +242,30 @@
         if cs > 1:
             lax.fori_loop(0, zs, other_core, 0)
 
-    def group_sum(value, buf, me, send, recv, peers):
-        if not peers:
-            return value
-        buf[me] = value
+    xy_sends = [(k, peer) for k, peer in enumerate(xy_ids)]
+    zc_sends = [(dc * zs + send_order[n], zc_peer(dc, send_order[n]))
+                for n in reversed(range(zs)) for dc in range(cs) if n + dc]
+
+    def group_start(value, buf, me, send, recv, peers):
+        buf[me] = value.astype(buf.dtype)
         copies = []
-        for k, peer in enumerate(peers):
+        for k, peer in peers:
             copy = remote(buf.at[me], buf.at[me], send.at[k], recv.at[k], peer)
             copy.start()
             copies.append(copy)
+        pending.extend(copies)
+        return copies
+
+    def group_finish(copies, buf):
         for copy in copies:
             copy.wait_recv()
-        pending.extend(copies)
-        total = buf[0]
+        total = buf[0].astype(F32)
         for slot in range(1, buf.shape[0]):
-            total = total + buf[slot]
+            total = total + buf[slot].astype(F32)
         return total
+
+    def group_sum(value, buf, me, send, recv, peers):
+        return group_finish(group_start(value, buf, me, send, recv, peers), buf)
 
     for copy in mass_copies:
         copy.wait_recv()
@@ -269,10 +278,13 @@
         mass_q = mine if mass_q is None else jnp.where(xi == x, mine, mass_q)
 
     def men_update(it, row_sum):
-        return men_mass / group_sum(row_sum, r_buf.at[it], xy_me, rx_s.at[it], rx_r.at[it], xy_ids)
-
-    def women_update(it, partial):
-        return mass_q / group_sum(partial, c_buf.at[it], zc_me, cz_s.at[it], cz_r.at[it], zc_ids)
+        return men_mass / group_sum(row_sum, r_buf.at[it], xy_me, rx_s.at[it], rx_r.at[it], xy_sends)
+
+    def women_start(it, partial):
+        return group_start(partial, c_buf.at[it], zc_me, cz_s.at[it], cz_r.at[it], zc_sends)
+
+    def women_finish(it, copies):
+        return mass_q / group_finish(copies, c_buf.at[it])
 
     zeros13 = jnp.zeros((13, group_rows), BF16)
     zeros13w = jnp.zeros((13, wb), BF16)
@@ -288,15 +300,17 @@
     total = lax.dot_general(jnp.ones((16, 2 * lanes), BF16), jnp.concatenate([high, low], axis=1),
                             RHS_T, preferred_element_type=F32)
     scale = men_update(0, total[0:1])
-    left0 = jnp.concatenate(list(split3(scale)) + [zeros13], axis=0)
-
-    def col_step(q, carry):
-        out = jnp.dot(left0, e_ref[q], preferred_element_type=F32)
-        col_ref[q:q + 1, :] = out[0:1] + out[1:2] + out[2:3]
-        return carry
-
-    sweep(col_step, 0)
-    col_ref[...] = women_update(0, col_ref[...])
+
+    def col_sweep(scale):
+        left = jnp.concatenate(list(split3(scale)) + [zeros13], axis=0)
+        for q in range(nb):
+            out = jnp.dot(left, e_ref[q], preferred_element_type=F32)
+            col_ref[q:q + 1, :] = out[0:1] + out[1:2] + out[2:3]
+        return col_ref[...]
+
+    sums = col_sweep(scale)
+    sent = women_start(0, sums)
+    col_ref[...] = women_finish(0, sent)
 
     def row_step(q, total):
         lines = jnp.concatenate(list(split3(col_ref[q:q + 1, :])) + [zeros13w], axis=0)
@@ -304,22 +318,24 @@
 
     total = sweep(row_step, jnp.zeros((16, group_rows), F32))
     scale = men_update(1, total[0:1] + total[1:2] + total[2:3])
+    sums = col_sweep(scale)
+    sent = women_start(1, sums)
     for x in range(xs):
         scale_ref[x] = scale[:, x * rows:(x + 1) * rows]
     ms_out[...] = scale_ref[xi]
-
     weighted = (men_full.astype(F32) * scale).astype(BF16)
-    left = jnp.concatenate([weighted] + list(split3(scale)) + [zeros13], axis=0)
-
-    def both_step(q, carry):
-        out = jnp.dot(left, e_ref[q], preferred_element_type=F32)
-        t_ref[q] = out[0:traits]
-        col_ref[q:q + 1, :] = (out[traits:traits + 1] + out[traits + 1:traits + 2]
-                               + out[traits + 2:traits + 3])
-        return carry
-
-    sweep(both_step, 0)
-    women_scale = women_update(1, col_ref[...])
+    share = traits // cs
+    for q in range(nb):
+        out = jnp.dot(weighted, e_ref[q], preferred_element_type=F32)
+        for part in range(cs):
+            t_ref[part, q] = out[part * share:(part + 1) * share]
+    swaps = []
+    if cs > 1:
+        copy = remote(t_ref.at[plus(ci, 1, cs)], t_in, tx_s.at[0], tx_r.at[0], zc_peer(1, 0))
+        copy.start()
+        swaps.append(copy)
+    pending.extend(swaps)
+    women_scale = women_finish(1, sent)
     col_ref[...] = women_scale
     wx_buf[xi] = women_scale
     wx_copies = []
@@ -329,19 +345,25 @@
         wx_copies.append(copy)
     pending.extend(wx_copies)
 
+    for copy in swaps:
+        copy.wait_recv()
+
     def moment_step(q, moment):
-        inner = t_ref[q] * col_ref[q:q + 1, :]
+        inner = t_ref[ci, q]
+        if cs > 1:
+            inner = inner + t_in[q]
+        inner = inner * col_ref[q:q + 1, :]
         high = inner.astype(BF16)
         low = (inner - high.astype(F32)).astype(BF16)
         both = jnp.concatenate([high, low], axis=0)
         return moment + lax.dot_general(both, wom_buf[q, 0:traits], RHS_T, preferred_element_type=F32)
 
-    moment = sweep(moment_step, jnp.zeros((2 * traits, traits), F32))
-    moment = moment[0:traits] + moment[traits:]
-    half = traits // 2
+    moment = sweep(moment_step, jnp.zeros((2 * share, traits), F32))
+    moment = moment[0:share] + moment[share:]
+    half = share // 2
     packed = jnp.concatenate([moment[0:half], moment[half:]], axis=1)
-    packed = group_sum(packed, mxy_buf, xy_me, rx_s.at[2], rx_r.at[2], xy_ids)
-    packed = group_sum(packed, mc_buf, ci, mc_s, mc_r, c_ids)
+    packed = group_sum(packed, mxy_buf, xy_me, rx_s.at[2], rx_r.at[2], xy_sends)
+    sent = group_start(packed, mz_buf, zc_me, mz_s, mz_r, zc_sends)
     for copy in wx_copies:
         copy.wait_recv()
     for x in range(xs):
@@ -349,8 +371,15 @@
         for q in range(nb):
             p = ((q % zs) * xs + x) * cs + q // zs
             ws_out[:, p * wb:(p + 1) * wb] = scales[q:q + 1, :]
-    packed = group_sum(packed, mz_buf, zi, mz_s, mz_r, z_ids)
-    moment = jnp.concatenate([packed[:, 0:traits], packed[:, traits:]], axis=0)
+    for copy in sent:
+        copy.wait_recv()
+    parts = []
+    for part in range(cs):
+        packed = mz_buf[part * zs]
+        for z in range(1, zs):
+            packed = packed + mz_buf[part * zs + z]
+        parts += [packed[:, 0:traits], packed[:, traits:]]
+    moment = jnp.concatenate(parts, axis=0)
     up_out[...] = aff_ref[...] + obs_ref[...] - moment * (1.0 / men_total)
 
     for copy in pending:
@@ -389,7 +418,7 @@
         dma = pltpu.SemaphoreType.DMA
         vmem = pl.BlockSpec(memory_space=pltpu.VMEM)
         anywhere = pl.BlockSpec(memory_space=pl.ANY)
-        packed = (traits // 2, 2 * traits)
+        packed = (traits // cs // 2, 2 * traits)
         out = pl.pallas_call(
             functools.partial(body, dims, women_axis, rows * men_axis, cols * women_axis),
             out_shape=(
@@ -404,20 +433,21 @@
                 pltpu.VMEM((nb, deep, wb), BF16),
                 pltpu.VMEM((nm * mb, deep), BF16),
                 pltpu.VMEM((nb, nm * mb, wb), BF16),
-                pltpu.VMEM((nb, traits, wb), F32),
+                pltpu.VMEM((cs, nb, traits // cs, wb), F32),
                 pltpu.VMEM((nb, wb), F32),
                 pltpu.VMEM((nm * mb, wb if wb % 128 else 128), F32),
                 pltpu.VMEM((xs, 1, rows), F32),
+                pltpu.VMEM((deep, 3 * traits), BF16),
                 pltpu.VMEM((traits, traits), F32),
                 pltpu.VMEM((traits, traits), F32),
                 pltpu.VMEM((1, cols), F32),
                 pltpu.VMEM((xs, 1, rows), F32),
                 pltpu.VMEM((xs, nb, wb), F32),
                 pltpu.VMEM((2, nm, 1, nm * mb), F32),
-                pltpu.VMEM((2, nb, nb, wb), F32),
+                pltpu.VMEM((2, nb, nb, wb), BF16),
                 pltpu.VMEM((nm,) + packed, F32),
-                pltpu.VMEM((cs,) + packed, F32),
-                pltpu.VMEM((zs,) + packed, F32),
+                pltpu.VMEM((nb,) + packed, F32),
+                pltpu.VMEM((nb, traits // cs, wb), F32),
                 dma((6,)),
                 dma((nm,)), dma((nm,)),
                 dma((zs,)), dma((zs,)),
@@ -426,8 +456,8 @@
                 dma((xs,)), dma((xs,)),
                 dma((3, nm)), dma((3, nm)),
                 dma((2, nb)), dma((2, nb)),
-                dma((cs,)), dma((cs,)),
-                dma((zs,)), dma((zs,)),
+                dma((1,)), dma((1,)),
+                dma((nb,)), dma((nb,)),
             ],
             compiler_params=pltpu.CompilerParams(
                 collective_id=0, has_side_effects=True, vmem_limit_bytes=60 * 1024 * 1024),

time: 43.3 us -> 41.8 us (0.965)
  Pallas kernels: 42.5 us -> 41 us
    pallas_call x1, Pallas kernels: 41.8 us -> 40.3 us  [on_device(): pl.pallas_call(functools.partial(body, dims, women_axis, rows * men_axis,...]
where the time goes in v2:
time: 41.8 us; the launch traced here: 41.6 us
  Pallas kernels  41 us (98%)
  between operations  0.64 us (2%)
    pallas_call x1, Pallas kernels, on_device(): pl.pallas_call(functools.partial(body, dims, women_axis, rows * men_axis,...  40.3 us

profile of v2, /device:TPU:0, one launch (start us, length us, event | category | flops | bytes accessed | tf_op | source)
XLA Modules:
  0.0 41.6 jit_solution(11430051745795948830)
XLA Ops:
  0.6 40.3 %shard_map.85 = (f32[1,1024]{1,0:T(1,128)S(1)}, f32[1,4096]{1,0:T(1,128)S(1)}, f32[64,64]{1,0:T(8,128)S(1)}) custom-call(bf16[64,512]{1,0:T(8,128)(2,1)} %men_ref.1, bf16[64,256]{1,0:T(8,128)(2,1)} %women_ref.1, f32[64,64]{1,0:T(8,128)} %aff_hbm.1, f32[64,64]{1,0:T(8,128)} %obs_hbm.1, f32[1,1024]{1,0:T(1,128)} %bitcast.5, f32[1,4096]{1,0:T(1,128)} %bitcast.4), custom_call_target="tpu_custom_call" | custom-call | tf_op jit(solution)/shard_map/pallas_call | solution.py:422
  41.0 0.7 %shard_map.86 = (f32[1,1024]{1,0:T(1,128)}, f32[1,4096]{1,0:T(1,128)}, f32[64,64]{1,0:T(8,128)}) custom-call(f32[1,1024]{1,0:T(1,128)S(1)} %get-tuple-element.9.ms_ref, f32[1,4096]{1,0:T(1,128)S(1)} %get-tuple-element.10.ws_ref, f32[64,64]{1,0:T(8,128)S(1)} %get-tuple-element.11.up_ref), custom_call_target="tpu_custom_call" | custom-call | tf_op jit(solution)/shard_map/pallas_call | solution.py:466

commit v3 on v2

--- a/solution.py
+++ b/solution.py
@@ -35,7 +35,7 @@
 def body(dims, ws, men_total, women_total,
          men_ref, women_ref, aff_hbm, obs_hbm, mm_hbm, wm_hbm,
          ms_out, ws_out, up_out,
-         men_buf, wom_buf, scaled_ref, e_ref, t_ref, col_ref, rsum_ref, scale_ref,
+         men_buf, wom_buf, scaled_ref, tall_ref, e_ref, et_ref, t_ref, col_ref, rsum_ref, scale_ref,
          left_aff, aff_ref, obs_ref, wm_ref, mass_buf, wx_buf,
          r_buf, c_buf, mxy_buf, mz_buf, t_in,
          own_sem, gm_s, gm_r, gz_s, gz_r, gc_s, gc_r, mm_s, mm_r, wx_s, wx_r,
@@ -90,7 +90,7 @@
             device_id=peer, device_id_type=MESH)
 
     def z_copy(dz):
-        return remote(women_ref, traits_of(zc_me), gz_s.at[dz], gz_r.at[dz], zc_peer(0, dz))
+        return remote(traits_of(zc_me), traits_of(zc_me), gz_s.at[dz], gz_r.at[dz], zc_peer(0, dz))
 
     def source_z(dz):
         return plus(zi, zs - dz, zs)
@@ -100,7 +100,7 @@
         return remote(held, held, gc_s.at[dz], gc_r.at[dz], zc_peer(1, 0))
 
     def m_copy(k):
-        return remote(men_ref, men_buf.at[xy_me], gm_s.at[k], gm_r.at[k],
+        return remote(men_buf.at[xy_me], men_buf.at[xy_me], gm_s.at[k], gm_r.at[k],
                       xy_peer(lax.div(k, ws), lax.rem(k, ws)))
 
     def by_distance(sign):
@@ -115,13 +115,16 @@
         return order
 
     order, send_order = by_distance(-1), by_distance(1)
-    first_copy = remote(women_ref, traits_of(zc_me), gc_s.at[0], gc_r.at[0], zc_peer(1, 0)) if cs > 1 else None
+    first_copy = remote(traits_of(zc_me), traits_of(zc_me), gc_s.at[0], gc_r.at[0], zc_peer(1, 0)) if cs > 1 else None
     pl.semaphore_wait(barrier, len(everyone))
+    local[0].wait()
+    local[1].wait()
     if cs > 1:
         first_copy.start()
     for n in range(1, zs):
         z_copy(send_order[n]).start()
-    for k in range(1, nm):
+    late = [nm - 1] if cs == 2 and nm == 4 and zs == 4 else []
+    for k in range(1, nm - len(late)):
         m_copy(k).start()
     pending = []
     for k, peer in enumerate(x_ids):
@@ -143,7 +146,9 @@
     def make_scaled(shard):
         block = men_buf[shard]
         tall = jnp.dot(left_aff[...], jnp.concatenate([block] * 3, axis=0), preferred_element_type=F32)
-        scaled_ref[rows_of(shard), :] = jnp.transpose(tall + ones_column).astype(BF16)
+        tall = tall + ones_column
+        tall_ref[shard] = tall.astype(BF16)
+        scaled_ref[rows_of(shard), :] = jnp.transpose(tall).astype(BF16)
 
     def fill(blocks, start, count):
         for part in range(count):
@@ -175,7 +180,7 @@
     for q in range(nb):
         wom_buf[q, traits:] = tail
     rsum_ref[...] = jnp.zeros_like(rsum_ref)
-    for copy in local:
+    for copy in local[2:]:
         copy.wait()
     wide = jnp.concatenate(split3(jnp.transpose(aff_ref[...])), axis=1)
     left_aff[...] = jnp.concatenate([wide, jnp.zeros((deep - traits, 3 * traits), BF16)], axis=0)
@@ -193,27 +198,33 @@
             z_copy(order[n]).wait_recv()
             c_copy(order[n]).start()
 
-        def take_men(k):
-            m_copy(k).wait_recv()
-            make_scaled(shard_of(k))
+        def cells(blocks, ks):
+            for k in ks:
+                fill(blocks, shard_of(k) * mb, mb // tile)
 
         c_copy(0).wait_recv()
-        fill_men([twin_block(0)], [0])
+        cells([twin_block(0)], [0])
+        m_copy(3).start()
         take_z(1)
-        fill_men([own_block(1)], [0])
-        take_men(2)
-        fill_men([own_block(0), twin_block(0), own_block(1)], [2])
+        cells([own_block(1)], [0])
+        m_copy(2).wait_recv()
         take_z(2)
+        cells([own_block(2)], [0])
+        make_scaled(shard_of(2))
         c_copy(order[1]).wait_recv()
-        fill_men([twin_block(1)], [0, 2])
-        take_men(1)
-        fill_men([own_block(0), twin_block(0), own_block(1), twin_block(1)], [1])
+        m_copy(1).wait_recv()
+        early = [own_block(0), twin_block(0), own_block(1), own_block(2), twin_block(1)]
+        cells(early, [2])
+        cells([twin_block(1)], [0])
+        make_scaled(shard_of(1))
         take_z(3)
-        fill_men([own_block(2)], [0, 1, 2])
-        take_men(3)
-        fill_men([own_block(0), twin_block(0), own_block(1), twin_block(1), own_block(2)], [3])
+        m_copy(3).wait_recv()
+        cells(early + [own_block(3)], [1])
+        cells([own_block(3)], [0, 2])
+        make_scaled(shard_of(3))
         c_copy(order[2]).wait_recv()
-        fill([twin_block(2), own_block(3)], 0, group_rows // tile)
+        cells(early + [own_block(3), twin_block(2)], [3])
+        cells([twin_block(2)], [0, 1, 2])
         c_copy(order[3]).wait_recv()
         fill([twin_block(3)], 0, group_rows // tile)
     else:
@@ -242,7 +253,7 @@
         if cs > 1:
             lax.fori_loop(0, zs, other_core, 0)
 
-    xy_sends = [(k, peer) for k, peer in enumerate(xy_ids)]
+    xy_sends = [(k, peer) for k, peer in enumerate(xy_ids)][::-1]
     zc_sends = [(dc * zs + send_order[n], zc_peer(dc, send_order[n]))
                 for n in reversed(range(zs)) for dc in range(cs) if n + dc]
 
@@ -277,8 +288,22 @@
         mine = jnp.concatenate([wm_ref[:, p * wb:(p + 1) * wb] for p in order], axis=0)
         mass_q = mine if mass_q is None else jnp.where(xi == x, mine, mass_q)
 
-    def men_update(it, row_sum):
-        return men_mass / group_sum(row_sum, r_buf.at[it], xy_me, rx_s.at[it], rx_r.at[it], xy_sends)
+    def men_start(it, row_sum):
+        return group_start(row_sum, r_buf.at[it], xy_me, rx_s.at[it], rx_r.at[it], xy_sends)
+
+    def men_finish(it, copies):
+        return men_mass / group_finish(copies, r_buf.at[it])
+
+    def mirror(first, last):
+        def one(q, carry):
+            block = jnp.transpose(wom_buf[q].astype(F32)).astype(BF16)
+            at = pl.ds(pl.multiple_of(q * wb, wb), wb)
+            for k in range(nm):
+                surplus = jnp.dot(block, tall_ref[k], preferred_element_type=F32)
+                et_ref[k, at, :] = jnp.exp(surplus).astype(BF16)
+            return carry
+
+        lax.fori_loop(first, last, one, 0)
 
     def women_start(it, partial):
         return group_start(partial, c_buf.at[it], zc_me, cz_s.at[it], cz_r.at[it], zc_sends)
@@ -287,7 +312,6 @@
         return mass_q / group_finish(copies, c_buf.at[it])
 
     zeros13 = jnp.zeros((13, group_rows), BF16)
-    zeros13w = jnp.zeros((13, wb), BF16)
 
     def sweep(step, carry):
         for q in range(nb):
@@ -299,7 +323,9 @@
     low = (sums - high.astype(F32)).astype(BF16)
     total = lax.dot_general(jnp.ones((16, 2 * lanes), BF16), jnp.concatenate([high, low], axis=1),
                             RHS_T, preferred_element_type=F32)
-    scale = men_update(0, total[0:1])
+    sent = men_start(0, total[0:1])
+    mirror(0, 3 * nb // 8)
+    scale = men_finish(0, sent)
 
     def col_sweep(scale):
         left = jnp.concatenate(list(split3(scale)) + [zeros13], axis=0)
@@ -310,14 +336,15 @@
 
     sums = col_sweep(scale)
     sent = women_start(0, sums)
-    col_ref[...] = women_finish(0, sent)
-
-    def row_step(q, total):
-        lines = jnp.concatenate(list(split3(col_ref[q:q + 1, :])) + [zeros13w], axis=0)
-        return total + lax.dot_general(lines, e_ref[q], RHS_T, preferred_element_type=F32)
-
-    total = sweep(row_step, jnp.zeros((16, group_rows), F32))
-    scale = men_update(1, total[0:1] + total[1:2] + total[2:3])
+    mirror(3 * nb // 8, nb)
+    women_scale = women_finish(0, sent)
+
+    spread = jnp.concatenate([women_scale[q:q + 1] for q in range(nb)], axis=1)
+    lines = jnp.concatenate(list(split3(spread)) + [jnp.zeros((13, nb * wb), BF16)], axis=0)
+    total = jnp.concatenate(
+        [jnp.dot(lines, et_ref[k], preferred_element_type=F32) for k in range(nm)], axis=1)
+    sent = men_start(1, total[0:1] + total[1:2] + total[2:3])
+    scale = men_finish(1, sent)
     sums = col_sweep(scale)
     sent = women_start(1, sums)
     for x in range(xs):
@@ -432,7 +459,9 @@
                 pltpu.VMEM((nm, traits, mb), BF16),
                 pltpu.VMEM((nb, deep, wb), BF16),
                 pltpu.VMEM((nm * mb, deep), BF16),
+                pltpu.VMEM((nm, deep, mb), BF16),
                 pltpu.VMEM((nb, nm * mb, wb), BF16),
+                pltpu.VMEM((nm, nb * wb, mb), BF16),
                 pltpu.VMEM((cs, nb, traits // cs, wb), F32),
                 pltpu.VMEM((nb, wb), F32),
                 pltpu.VMEM((nm * mb, wb if wb % 128 else 128), F32),

time: 41.8 us -> 40.2 us (0.962)
  Pallas kernels: 41 us -> 39.4 us
    pallas_call x1, Pallas kernels: 40.3 us -> 38.8 us  [on_device(): pl.pallas_call(functools.partial(body, dims, women_axis, rows * men_axis,...]
where the time goes in v3:
time: 40.2 us; the launch traced here: 40.1 us
  Pallas kernels  39.4 us (98%)
  between operations  0.64 us (2%)
    pallas_call x1, Pallas kernels, on_device(): pl.pallas_call(functools.partial(body, dims, women_axis, rows * men_axis,...  38.8 us

profile of v3, /device:TPU:0, one launch (start us, length us, event | category | flops | bytes accessed | tf_op | source)
XLA Modules:
  0.0 40.1 jit_solution(12507355517309423266)
XLA Ops:
  0.6 38.8 %shard_map.85 = (f32[1,1024]{1,0:T(1,128)S(1)}, f32[1,4096]{1,0:T(1,128)S(1)}, f32[64,64]{1,0:T(8,128)S(1)}) custom-call(bf16[64,512]{1,0:T(8,128)(2,1)} %men_ref.1, bf16[64,256]{1,0:T(8,128)(2,1)} %women_ref.1, f32[64,64]{1,0:T(8,128)} %aff_hbm.1, f32[64,64]{1,0:T(8,128)} %obs_hbm.1, f32[1,1024]{1,0:T(1,128)} %bitcast.5, f32[1,4096]{1,0:T(1,128)} %bitcast.4), custom_call_target="tpu_custom_call" | custom-call | tf_op jit(solution)/shard_map/pallas_call | solution.py:449
  39.4 0.7 %shard_map.86 = (f32[1,1024]{1,0:T(1,128)}, f32[1,4096]{1,0:T(1,128)}, f32[64,64]{1,0:T(8,128)}) custom-call(f32[1,1024]{1,0:T(1,128)S(1)} %get-tuple-element.9.ms_ref, f32[1,4096]{1,0:T(1,128)S(1)} %get-tuple-element.10.ws_ref, f32[64,64]{1,0:T(8,128)S(1)} %get-tuple-element.11.up_ref), custom_call_target="tpu_custom_call" | custom-call | tf_op jit(solution)/shard_map/pallas_call | solution.py:495
